TPU v7x, 32 devices: a whole 2x2x4 slice. The times are simulated.
32 devices in a mesh: parts: 2 (over y), blk: 4 (over z), grp: 4 (over x, core).
Axes of the slice: x: 2, y: 2, z: 4, core: 2. Of those that a mesh axis runs over, the one named last changes fastest.
Arguments:
- factors: float32 [64, 4096], P(None, ('parts', 'blk', 'grp')), parts along dimension 1, may hold values from -1 to 1
- tangent: float32 [64, 4096], P(None, ('parts', 'blk', 'grp')), parts along dimension 1, may hold values from -15 to 15
- counts: int32 [4096, 2048], P(('parts', 'blk', 'grp')), parts along dimension 0, may hold values from 0 to 4, as said below
Outputs:
- hess_vec: float32 [64, 4096], P(None, ('parts', 'blk', 'grp')), parts along dimension 1
- residual: float32 [64, 4096], P(None, ('parts', 'blk', 'grp')), parts along dimension 1
- inner: float32 [4], P('parts'), parts along dimension 0
There are 2 independent parts, one for each index of `parts`. A program takes and returns all parts, laid end to end along the dimension named above; each array names one. Nothing has to cross between parts.
Inputs may be any that keep to these rules, and one draw needn't show every extreme that they name: counts is symmetric.
All inputs are finite; a program needn't handle non-finite values.
Results may differ from a plain program's by a relative error of at most 0.0003.
Values sent between devices are 32-bit elements; how exact they have to be, the bound alone decides.
A program may use at most 128 MiB of HBM per device.

v0:
```python
import jax
import jax.numpy as jnp
from jax import lax
from jax.sharding import PartitionSpec as P


def local(factors, tangent, counts):
    rows = counts.shape[0]
    nodes = counts.shape[1]
    scale = 1.0 / jnp.sqrt(jnp.float32(nodes))
    highest = lax.Precision.HIGHEST
    contract = (((0,), (0,)), ((), ()))
    right = (((1,), (1,)), ((), ()))
    row_start = (lax.axis_index("blk") * lax.axis_size("grp") + lax.axis_index("grp")) * rows
    row_ids = row_start + jnp.arange(rows, dtype=jnp.int32)[:, None]
    group_u, group_v = (
        lax.all_gather(factors, "grp", axis=1, tiled=True),
        lax.all_gather(tangent, "grp", axis=1, tiled=True),
    )
    piece_u = lax.all_gather(group_u, "blk", axis=1, tiled=True)
    piece_v = lax.all_gather(group_v, "blk", axis=1, tiled=True)
    width = piece_u.shape[1]
    eta = lax.dot_general(factors, piece_u, contract, precision=highest)
    deta = lax.dot_general(factors, piece_v, contract, precision=highest) + lax.dot_general(
        tangent, piece_u, contract, precision=highest
    )
    col_ids = jnp.arange(width, dtype=jnp.int32)[None, :]
    keep = row_ids != col_ids
    rate = jnp.where(keep, jnp.exp(eta), jnp.float32(0.0))
    weight = rate * deta
    tile_counts = counts.astype(jnp.float32)
    slack = jnp.where(keep, tile_counts - rate, jnp.float32(0.0))
    hess_acc = lax.dot_general(piece_u, weight, right, precision=highest)
    resid_acc = lax.dot_general(piece_u, slack - weight, right, precision=highest)
    hess_acc, resid_acc = (hess_acc, resid_acc)
    hess_vec = hess_acc * scale
    residual = resid_acc * scale
    sum_sq, sum_curv = lax.psum(
        (jnp.sum(residual * residual), jnp.sum(tangent * hess_vec)), ("blk", "grp")
    )
    inner = jnp.stack([sum_sq, sum_curv])
    return (hess_vec, residual, inner)


def solution(mesh):
    return jax.shard_map(
        local,
        mesh=mesh,
        in_specs=(
            P(None, ("parts", "blk", "grp")),
            P(None, ("parts", "blk", "grp")),
            P(("parts", "blk", "grp"), None),
        ),
        out_specs=(P(None, ("parts", "blk", "grp")), P(None, ("parts", "blk", "grp")), P("parts")),
        check_vma=False,
    )
```

profile of v0, /device:TPU:0, one launch (start us, length us, event | category | flops | bytes accessed | tf_op | source)
XLA Modules:
  0.0 85.9 jit_solution(17943244656120877728)
XLA Ops:
  0.6 0.0 copy-start.1
  0.7 6.7 %all_gather.12 = f32[64,512]{1,0:T(8,128)S(1)} all-gather(f32[64,128]{1,0:T(8,128)} %param.3), channel_id=1, replica_groups=mesh['parts'=2,'blk'=4,'grp'=4] {'grp'}, dimensions={1}, use_global_device_ids=true | all-gather | bytes 163840 | tf_op jit(solution)/shard_map/all_gather | solution.py:17
  7.4 0.0 copy-done.1
  7.4 5.6 %all_gather.14 = f32[64,512]{1,0:T(8,128)S(1)} all-gather(f32[64,128]{1,0:T(8,128)S(1)} %copy-done.1), channel_id=1, replica_groups=mesh['parts'=2,'blk'=4,'grp'=4] {'grp'}, dimensions={1}, use_global_device_ids=true | all-gather | bytes 163840 | tf_op jit(solution)/shard_map/all_gather | solution.py:18
  12.9 16.6 %all_gather.13 = f32[64,2048]{1,0:T(8,128)S(1)} all-gather(f32[64,512]{1,0:T(8,128)S(1)} %all_gather.12), channel_id=1, replica_groups=mesh['parts'=2,'blk'=4,'grp'=4] {'blk'}, dimensions={1}, use_global_device_ids=true | all-gather | bytes 655360 | tf_op jit(solution)/shard_map/all_gather | solution.py:20
  29.5 0.0 copy-start.2
  29.5 16.0 %all_gather.15 = f32[64,2048]{1,0:T(8,128)S(1)} all-gather(f32[64,512]{1,0:T(8,128)S(1)} %all_gather.14), channel_id=1, replica_groups=mesh['parts'=2,'blk'=4,'grp'=4] {'blk'}, dimensions={1}, use_global_device_ids=true | all-gather | bytes 655360 | tf_op jit(solution)/shard_map/all_gather | solution.py:21
  45.5 0.0 copy-done.2
  45.5 1.0 %fusion.11 = f32[128,2048]{1,0:T(8,128)S(1)} fusion(f32[64,128]{1,0:T(8,128)S(1)} %copy-done.2, f32[64,2048]{1,0:T(8,128)S(1)} %all_gather.15), kind=kOutput, calls=%fused_computation.20 | convolution fusion | flops 201326592 | bytes 1605632 | tf_op jit(solution)/shard_map/dot_general | solution.py:24
  46.6 1.1 %fusion.1 = f32[128,2048]{1,0:T(8,128)S(1)} fusion(f32[64,128]{1,0:T(8,128)S(1)} %copy-done.2, f32[64,2048]{1,0:T(8,128)S(1)} %all_gather.13, s32[128]{0:T(128)S(1)} %iota_add_fusion), kind=kOutput, calls=%fused_computation.3 | convolution fusion | flops 201850880 | bytes 1606144 | tf_op jit(solution)/shard_map/dot_general | solution.py:23
  47.7 0.0 copy-start
  47.7 1.1 %fusion = f32[128,2048]{1,0:T(8,128)S(1)} fusion(f32[128,2048]{1,0:T(8,128)S(1)} %fusion.1, f32[128,2048]{1,0:T(8,128)S(1)} %fusion.11, f32[64,128]{1,0:T(8,128)S(1)} %copy-done.1, f32[64,2048]{1,0:T(8,128)S(1)} %all_gather.13), kind=kOutput, calls=%fused_computation.1 | convolution fusion | flops 201850880 | bytes 3702784 | tf_op jit(solution)/shard_map/dot_general | solution.py:24
  48.8 0.2 copy-done
  48.9 2.7 %multiply_reduce_fusion.1 = (f32[]{:T(128)}, f32[64,128]{1,0:T(8,128)}) fusion(f32[64,2048]{1,0:T(8,128)S(1)} %all_gather.13, f32[128,2048]{1,0:T(8,128)S(1)} %fusion, f32[128,2048]{1,0:T(8,128)S(1)} %fusion.1, s32[128,2048]{1,0:T(8,128)S(1)} %copy-done, s32[128]{0:T(128)S(1)} %iota_add_fusion), kind=kOutput, calls=%fused_computation.16 | convolution fusion | flops 202661888 | bytes 3703300 | tf_op jit(solution)/shard_map/dot_general | solution.py:34
  51.6 2.4 %multiply_reduce_fusion = (f32[]{:T(128)}, f32[64,128]{1,0:T(8,128)}) fusion(f32[64,128]{1,0:T(8,128)S(1)} %copy-done.1, f32[128,2048]{1,0:T(8,128)S(1)} %fusion, f32[64,2048]{1,0:T(8,128)S(1)} %all_gather.13), kind=kOutput, calls=%fused_computation.15 | convolution fusion | flops 201351168 | bytes 1638404 | tf_op jit(solution)/shard_map/dot_general | solution.py:33
  54.0 30.1 %all-reduce = (f32[1]{0:T(128)}, f32[1]{0:T(128)}) all-reduce(f32[1]{0:T(128)} %bitcast.3, f32[1]{0:T(128)} %bitcast.2), channel_id=1, replica_groups=mesh['parts'=2,'blk'=4,'grp'=4] {'blk','grp'}, use_global_device_ids=true, to_apply=%region_3.4 | all-reduce | flops 2 | bytes 16 | tf_op jit(solution)/shard_map/psum | solution.py:38
  84.2 1.8 %pad_maximum_fusion = f32[2]{0:T(128)} fusion(f32[1]{0:T(128)} %get-tuple-element.3, f32[1]{0:T(128)} %get-tuple-element.4), kind=kLoop, calls=%fused_computation.17 | loop fusion | flops 2 | bytes 16 | tf_op jit(solution)/shard_map/stack | solution.py:41
  (1 shorter events, 0.0 us)
Async XLA Ops:
  0.6 6.7 %copy-start.1 = (f32[64,128]{1,0:T(8,128)S(1)}, f32[64,128]{1,0:T(8,128)}, u32[]{:S(2)}) copy-start(f32[64,128]{1,0:T(8,128)} %param.4) | copy-start | bytes 98308
  29.5 16.0 %copy-start.2 = (f32[64,128]{1,0:T(8,128)S(1)}, f32[64,128]{1,0:T(8,128)}, u32[]{:S(2)}) copy-start(f32[64,128]{1,0:T(8,128)} %param.3) | copy-start | bytes 98308
  47.7 1.2 %copy-start = (s32[128,2048]{1,0:T(8,128)S(1)}, s32[128,2048]{1,0:T(8,128)}, u32[]{:S(2)}) copy-start(s32[128,2048]{1,0:T(8,128)} %param.5) | copy-start | bytes 3145732
where the time goes:
time: 86.3 us; the launch traced here: 85.9 us
  blocking collectives  75 us (87%)
  matrix products  8.3 us (10%)
  other arithmetic  1.78 us (2%)
    psum x1, blocking collectives, local(): lax.psum((jnp.sum(residual * residual), jnp.sum(tangent * hess_vec)), ('b...  30.1 us
    all_gather x1, blocking collectives, local(): piece_u = lax.all_gather(group_u, 'blk', axis=1, tiled=True)  16.6 us
    all_gather x1, blocking collectives, local(): piece_v = lax.all_gather(group_v, 'blk', axis=1, tiled=True)  16 us
    all_gather x1, blocking collectives, local(): lax.all_gather(factors, 'grp', axis=1, tiled=True)  6.69 us
    all_gather x1, blocking collectives, local(): lax.all_gather(tangent, 'grp', axis=1, tiled=True)  5.58 us
    dot_general x1, matrix products, local(): lax.dot_general(piece_u, slack - weight, right, precision=highest)  2.69 us
    dot_general x1, matrix products, local(): hess_acc = lax.dot_general(piece_u, weight, right, precision=highest)  2.41 us
    another operation x1, other arithmetic, local(): inner = jnp.stack([sum_sq, sum_curv])  1.78 us

commit v1 on v0

v1 whole, which is shorter than its diff:
```python
import functools

import jax
import jax.numpy as jnp
from jax import lax
from jax.experimental import pallas as pl
from jax.experimental.pallas import tpu as pltpu
from jax.sharding import PartitionSpec as P

MESH = pl.DeviceIdType.MESH


def split(x):
    hi = x.astype(jnp.bfloat16)
    lo = (x - hi.astype(jnp.float32)).astype(jnp.bfloat16)
    return hi, lo


def kernel(
    n_blk,
    n_grp,
    f_hbm,
    t_hbm,
    c_hbm,
    h_hbm,
    r_hbm,
    inner_ref,
    slots,
    counts,
    lhs,
    acc,
    h_buf,
    r_buf,
    stats,
    local_sem,
    z_sem,
    x_sem,
    s_sem,
    recv_sem,
    stat_send,
    stat_recv,
):
    n_x = n_grp // 2
    n_dev = n_blk * n_grp
    rank, rows = h_buf.shape
    nodes = counts.shape[1]
    blk = lax.axis_index("blk")
    grp = lax.axis_index("grp")
    x, core = grp // 2, lax.rem(grp, 2)
    me = blk * n_grp + grp
    sibling = 2 * x + 1 - core

    def peer(k):
        there = lax.rem(me + k, n_dev)
        return there, {"blk": there // n_grp, "grp": lax.rem(there, n_grp)}

    load_f = pltpu.make_async_copy(f_hbm, slots.at[me, pl.ds(0, rank)], local_sem.at[0])
    load_t = pltpu.make_async_copy(t_hbm, slots.at[me, pl.ds(rank, rank)], local_sem.at[1])
    load_c = pltpu.make_async_copy(c_hbm, counts, local_sem.at[2])
    load_f.start()
    load_t.start()
    load_c.start()

    barrier = pltpu.get_barrier_semaphore()

    @pl.loop(1, n_dev)
    def _(k):
        pl.semaphore_signal(barrier, inc=1, device_id=peer(k)[1], device_id_type=MESH)

    load_f.wait()
    load_t.wait()
    pl.semaphore_wait(barrier, n_dev - 1)

    def send(slot, b, g, sem):
        return pltpu.make_async_remote_copy(
            src_ref=slots.at[slot],
            dst_ref=slots.at[slot],
            send_sem=sem,
            recv_sem=recv_sem.at[slot],
            device_id={"blk": b, "grp": g},
            device_id_type=MESH,
        )

    def arrived(slot):
        send(slot, blk, sibling, s_sem.at[0]).wait_recv()

    def to_z(k):
        return send(me, lax.rem(blk + k, n_blk), grp, z_sem.at[k])

    def from_z(k):
        return lax.rem(blk + n_blk - k, n_blk)

    def x_at(dx):
        return lax.rem(x + dx, n_x)

    def to_x(k, dx):
        return send(from_z(k) * n_grp + grp, blk, 2 * x_at(dx) + core, x_sem.at[k, dx])

    def to_sibling(k, dx):
        return send(from_z(k) * n_grp + 2 * x_at(dx) + core, blk, sibling, s_sem.at[k * n_x + dx])

    def slot_own_core(k, dx):
        return from_z(k) * n_grp + 2 * x_at(dx) + core

    def slot_sibling(k, dx):
        return from_z(k) * n_grp + 2 * x_at(dx) + 1 - core

    for k in range(1, n_blk):
        to_z(k).start()
    for dx in range(1, n_x):
        to_x(0, dx).start()
    to_sibling(0, 0).start()

    u = slots[me, pl.ds(0, rank), :]
    v = slots[me, pl.ds(rank, rank), :]
    u_hi, u_lo = split(jnp.concatenate([u, jnp.zeros_like(u)], axis=0).T)
    d_hi, d_lo = split(jnp.concatenate([v, u], axis=0).T)
    for i, part in enumerate((u_hi, u_lo, d_hi, d_lo)):
        lhs[pl.ds(i * rows, rows), pl.ds(0, 2 * rank)] = part
        lhs[pl.ds(i * rows, rows), pl.ds(2 * rank, 2 * rank)] = part
    acc[...] = jnp.zeros_like(acc)
    load_c.wait()

    def tile(b, xx):
        pair = b * n_grp + 2 * xx
        width = 2 * rows
        start = pl.multiple_of(pair * rows, width)
        block = jnp.concatenate([slots[pair], slots[pair + 1]], axis=1)
        hi, lo = split(block)
        both = jnp.concatenate([hi, lo], axis=0)
        z = jnp.dot(lhs[...], both, preferred_element_type=jnp.float32)
        eta = z[:rows] + z[rows : 2 * rows]
        deta = z[2 * rows : 3 * rows] + z[3 * rows :]
        col = lax.broadcasted_iota(jnp.int32, (rows, width), 1)
        row = lax.broadcasted_iota(jnp.int32, (rows, width), 0)
        keep = (col - row) != (me - pair) * rows
        rate = jnp.where(keep, jnp.exp(eta), 0.0)
        weight = rate * deta
        c = counts[:, pl.ds(start, width)].astype(jnp.float32)
        slack = jnp.where(keep, c - rate, 0.0)
        w_hi, w_lo = split(weight)
        t_hi, t_lo = split(slack - weight)
        p = jnp.concatenate([w_hi, w_lo, t_hi, t_lo], axis=0)
        uu = jnp.concatenate([hi[:rank], lo[:rank]], axis=0)
        acc[...] += lax.dot_general(
            p, uu, (((1,), (1,)), ((), ())), preferred_element_type=jnp.float32
        )

    def step(k, _):
        @pl.when(k < n_blk)
        def _():
            @pl.when(k > 0)
            def _():
                arrived(slot_own_core(k, 0))
                for dx in range(1, n_x):
                    to_x(k, dx).start()
                to_sibling(k, 0).start()

        @pl.when(jnp.logical_and(k > 0, k <= n_blk))
        def _():
            for dx in range(1, n_x):
                arrived(slot_own_core(k - 1, dx))
                to_sibling(k - 1, dx).start()
            arrived(slot_sibling(k - 1, 0))
            tile(from_z(k - 1), x)

        @pl.when(k > 1)
        def _():
            @pl.loop(1, n_x)
            def _(dx):
                arrived(slot_sibling(k - 2, dx))
                tile(from_z(k - 2), x_at(dx))

        return 0

    lax.fori_loop(0, n_blk + 2, step, 0)

    scale = 1.0 / jnp.sqrt(jnp.float32(nodes))
    h = (acc[pl.ds(0, rows)] + acc[pl.ds(rows, rows)]).T
    r = (acc[pl.ds(2 * rows, rows)] + acc[pl.ds(3 * rows, rows)]).T
    h = (h[:rank] + h[rank:]) * scale
    r = (r[:rank] + r[rank:]) * scale
    h_buf[...] = h
    r_buf[...] = r
    sq = r * r
    curv = slots[me, pl.ds(rank, rank), :] * h
    stats[me, pl.ds(0, 8)] = jnp.sum(sq.reshape(rank // 8, 8, rows), axis=0)
    stats[me, pl.ds(8, 8)] = jnp.sum(curv.reshape(rank // 8, 8, rows), axis=0)

    def to_stat(k):
        return pltpu.make_async_remote_copy(
            src_ref=stats.at[me],
            dst_ref=stats.at[me],
            send_sem=stat_send.at[k],
            recv_sem=stat_recv.at[me],
            device_id=peer(k)[1],
            device_id_type=MESH,
        )

    def stat_arrived(k):
        there = peer(k)[0]
        pltpu.make_async_remote_copy(
            src_ref=stats.at[there],
            dst_ref=stats.at[there],
            send_sem=stat_send.at[0],
            recv_sem=stat_recv.at[there],
            device_id=peer(k)[1],
            device_id_type=MESH,
        ).wait_recv()

    @pl.loop(1, n_dev)
    def _(k):
        to_stat(k).start()

    store_h = pltpu.make_async_copy(h_buf, h_hbm, local_sem.at[0])
    store_r = pltpu.make_async_copy(r_buf, r_hbm, local_sem.at[1])
    store_h.start()
    store_r.start()

    @pl.loop(1, n_blk)
    def _(k):
        to_z(k).wait_send()

    @pl.loop(0, n_blk)
    def _(k):
        for dx in range(n_x):
            if dx > 0:
                to_x(k, dx).wait_send()
            to_sibling(k, dx).wait_send()

    @pl.loop(1, n_dev)
    def _(k):
        stat_arrived(k)

    total = jnp.sum(stats[...], axis=0)
    inner_ref[0] = jnp.sum(total[:8])
    inner_ref[1] = jnp.sum(total[8:])

    @pl.loop(1, n_dev)
    def _(k):
        to_stat(k).wait_send()

    store_h.wait()
    store_r.wait()


def local(n_blk, n_grp, factors, tangent, counts):
    rank, rows = factors.shape
    nodes = counts.shape[1]
    n_x = n_grp // 2
    n_dev = n_blk * n_grp
    anyspace = pl.BlockSpec(memory_space=pl.ANY)
    flat = jax.ShapeDtypeStruct((rank, rows), jnp.float32)
    return pl.pallas_call(
        functools.partial(kernel, n_blk, n_grp),
        out_shape=(flat, flat, jax.ShapeDtypeStruct((2,), jnp.float32)),
        in_specs=[anyspace] * 3,
        out_specs=(anyspace, anyspace, pl.BlockSpec(memory_space=pltpu.SMEM)),
        scratch_shapes=[
            pltpu.VMEM((n_dev, 2 * rank, rows), jnp.float32),
            pltpu.VMEM((rows, nodes), jnp.int32),
            pltpu.VMEM((4 * rows, 4 * rank), jnp.bfloat16),
            pltpu.VMEM((4 * rows, 2 * rank), jnp.float32),
            pltpu.VMEM((rank, rows), jnp.float32),
            pltpu.VMEM((rank, rows), jnp.float32),
            pltpu.VMEM((n_dev, 16, rows), jnp.float32),
            pltpu.SemaphoreType.DMA((3,)),
            pltpu.SemaphoreType.DMA((n_blk,)),
            pltpu.SemaphoreType.DMA((n_blk, n_x)),
            pltpu.SemaphoreType.DMA((n_dev,)),
            pltpu.SemaphoreType.DMA((n_dev,)),
            pltpu.SemaphoreType.DMA((n_dev,)),
            pltpu.SemaphoreType.DMA((n_dev,)),
        ],
        compiler_params=pltpu.CompilerParams(
            collective_id=0, has_side_effects=True, vmem_limit_bytes=64 * 1024 * 1024 - 64 * 1024
        ),
    )(factors, tangent, counts)


def solution(mesh):
    nodes = P(None, ("parts", "blk", "grp"))
    return jax.shard_map(
        functools.partial(local, mesh.shape["blk"], mesh.shape["grp"]),
        mesh=mesh,
        in_specs=(nodes, nodes, P(("parts", "blk", "grp"), None)),
        out_specs=(nodes, nodes, P("parts")),
        check_vma=False,
    )
```

time: 86.3 us -> 29.4 us (0.34)
  blocking collectives: 75 us -> 0 us
  Pallas kernels: 0 us -> 25.9 us
  matrix products: 8.3 us -> 0 us
  local copies, waits for them, and re-layouts: 0.17 us -> 2.57 us
  other arithmetic: 1.78 us -> 0 us
    all_gather x4 -> x0, blocking collectives: 44.9 us -> none  [the longest x1 16.6 us: local(): piece_u = lax.all_gather(group_u, 'blk', axis=1, tiled=True)]
    psum x1 -> x0, blocking collectives: 30.1 us -> none  [local(): lax.psum((jnp.sum(residual * residual), jnp.sum(tangent * hess_vec)), ('b...]
    pallas_call x0 -> x1, Pallas kernels: none -> 25.9 us  [local(): pl.pallas_call(functools.partial(kernel, n_blk, n_grp), out_shape=(flat,...]
    dot_general x5 -> x0, matrix products: 8.3 us -> none  [the longest x1 2.69 us: local(): lax.dot_general(piece_u, slack - weight, right, precision=highest)]
    unnamed x6 -> x7, local copies, waits for them, and re-layouts: 0.17 us -> 2.57 us
    another operation x1 -> x0, other arithmetic: 1.78 us -> none  [local(): inner = jnp.stack([sum_sq, sum_curv])]
where the time goes in v1:
time: 29.4 us; the launch traced here: 29.1 us
  Pallas kernels  25.9 us (88%)
  local copies, waits for them, and re-layouts  2.57 us (9%)
  between operations  0.65 us (2%)
    pallas_call x1, Pallas kernels, local(): pl.pallas_call(functools.partial(kernel, n_blk, n_grp), out_shape=(flat,...  25.9 us
    unnamed x7, local copies, waits for them, and re-layouts  2.57 us

profile of v1, /device:TPU:0, one launch (start us, length us, event | category | flops | bytes accessed | tf_op | source)
XLA Modules:
  0.0 29.1 jit_solution(15058743086783837935)
XLA Ops:
  0.6 25.9 %shard_map.58 = (f32[64,128]{1,0:T(8,128)}, f32[64,128]{1,0:T(8,128)}, f32[2]{0:T(128)}) custom-call(f32[64,128]{1,0:T(8,128)} %f_hbm.1, f32[64,128]{1,0:T(8,128)} %t_hbm.1, s32[128,2048]{1,0:T(8,128)} %c_hbm.1), custom_call_target="tpu_custom_call" | custom-call | tf_op jit(solution)/shard_map/pallas_call | solution.py:254
  26.6 0.0 copy-start
  26.6 1.4 %copy.9 = f32[64,128]{1,0:T(8,128)} copy(f32[64,128]{1,0:T(8,128)} %get-tuple-element.6) | data formatting | bytes 65536
  28.0 0.0 copy-done
  28.0 0.0 copy-start.1
  28.0 0.6 %copy.10 = f32[64,128]{1,0:T(8,128)} copy(f32[64,128]{1,0:T(8,128)S(1)} %copy-done) | data formatting | bytes 65536
  28.6 0.1 copy-done.1
  28.6 0.5 %copy.11 = f32[2]{0:T(128)} copy(f32[2]{0:T(128)S(1)} %copy-done.1) | data formatting | bytes 16
Async XLA Ops:
  26.6 1.4 %copy-start = (f32[64,128]{1,0:T(8,128)S(1)}, f32[64,128]{1,0:T(8,128)}, u32[]{:S(2)}) copy-start(f32[64,128]{1,0:T(8,128)} %get-tuple-element.7) | copy-start | bytes 98308
  28.0 0.7 %copy-start.1 = (f32[2]{0:T(128)S(1)}, f32[2]{0:T(128)}, u32[]{:S(2)}) copy-start(f32[2]{0:T(128)} %get-tuple-element.8) | copy-start | bytes 28

commit v2 on v1

--- a/solution.py
+++ b/solution.py
@@ -71,45 +71,46 @@
     load_t.wait()
     pl.semaphore_wait(barrier, n_dev - 1)
 
-    def send(slot, b, g, sem):
+    def send(slot, half, b, g, sem):
+        part = slots.at[slot, pl.ds(half * rank, rank)]
         return pltpu.make_async_remote_copy(
-            src_ref=slots.at[slot],
-            dst_ref=slots.at[slot],
+            src_ref=part,
+            dst_ref=part,
             send_sem=sem,
-            recv_sem=recv_sem.at[slot],
+            recv_sem=recv_sem.at[slot, half],
             device_id={"blk": b, "grp": g},
             device_id_type=MESH,
         )
 
-    def arrived(slot):
-        send(slot, blk, sibling, s_sem.at[0]).wait_recv()
-
-    def to_z(k):
-        return send(me, lax.rem(blk + k, n_blk), grp, z_sem.at[k])
-
-    def from_z(k):
-        return lax.rem(blk + n_blk - k, n_blk)
+    def arrived(slot, half):
+        send(slot, half, blk, sibling, s_sem.at[0, 0]).wait_recv()
 
     def x_at(dx):
         return lax.rem(x + dx, n_x)
 
-    def to_x(k, dx):
-        return send(from_z(k) * n_grp + grp, blk, 2 * x_at(dx) + core, x_sem.at[k, dx])
-
-    def to_sibling(k, dx):
-        return send(from_z(k) * n_grp + 2 * x_at(dx) + core, blk, sibling, s_sem.at[k * n_x + dx])
-
-    def slot_own_core(k, dx):
-        return from_z(k) * n_grp + 2 * x_at(dx) + core
-
-    def slot_sibling(k, dx):
-        return from_z(k) * n_grp + 2 * x_at(dx) + 1 - core
-
-    for k in range(1, n_blk):
-        to_z(k).start()
-    for dx in range(1, n_x):
-        to_x(0, dx).start()
-    to_sibling(0, 0).start()
+    def to_z(b, half, there, k):
+        return send(b * n_grp + grp, half, there, grp, z_sem.at[k, half])
+
+    def to_x(b, dx, half):
+        return send(b * n_grp + grp, half, blk, 2 * x_at(dx) + core, x_sem.at[b, dx, half])
+
+    def to_sibling(b, dx, half):
+        slot = b * n_grp + 2 * x_at(dx) + core
+        return send(slot, half, blk, sibling, s_sem.at[slot, half])
+
+    def inside(b):
+        return jnp.logical_and(b >= 0, b < n_blk)
+
+    for half in range(2):
+        for k, there in enumerate((blk - 1, blk + 1)):
+
+            @pl.when(inside(there))
+            def _():
+                to_z(blk, half, there, blk if k == 0 else n_blk).start()
+
+        for dx in range(1, n_x):
+            to_x(blk, dx, half).start()
+        to_sibling(blk, 0, half).start()
 
     u = slots[me, pl.ds(0, rank), :]
     v = slots[me, pl.ds(rank, rank), :]
@@ -147,29 +148,54 @@
         )
 
     def step(k, _):
-        @pl.when(k < n_blk)
-        def _():
-            @pl.when(k > 0)
+        for half in range(2):
+            for side in (-1, 1):
+                b = blk + side * k
+
+                @pl.when(jnp.logical_and(k > 0, inside(b)))
+                def _():
+                    arrived(b * n_grp + grp, half)
+
+                    @pl.when(inside(blk - side))
+                    def _():
+                        to_z(b, half, blk - side, b).start()
+
+                    for dx in range(1, n_x):
+                        to_x(b, dx, half).start()
+                    to_sibling(b, 0, half).start()
+
+        for half in range(2):
+            for side in (-1, 1):
+                b = blk + side * (k - 1)
+                first = jnp.logical_or(k > 1, side > 0)
+
+                @pl.when(jnp.logical_and(jnp.logical_and(k > 0, first), inside(b)))
+                def _():
+                    for dx in range(1, n_x):
+                        arrived(b * n_grp + 2 * x_at(dx) + core, half)
+                        to_sibling(b, dx, half).start()
+
+        for side in (-1, 1):
+            b = blk + side * (k - 1)
+            first = jnp.logical_or(k > 1, side > 0)
+
+            @pl.when(jnp.logical_and(jnp.logical_and(k > 0, first), inside(b)))
             def _():
-                arrived(slot_own_core(k, 0))
-                for dx in range(1, n_x):
-                    to_x(k, dx).start()
-                to_sibling(k, 0).start()
-
-        @pl.when(jnp.logical_and(k > 0, k <= n_blk))
-        def _():
-            for dx in range(1, n_x):
-                arrived(slot_own_core(k - 1, dx))
-                to_sibling(k - 1, dx).start()
-            arrived(slot_sibling(k - 1, 0))
-            tile(from_z(k - 1), x)
-
-        @pl.when(k > 1)
-        def _():
-            @pl.loop(1, n_x)
-            def _(dx):
-                arrived(slot_sibling(k - 2, dx))
-                tile(from_z(k - 2), x_at(dx))
+                arrived(b * n_grp + 2 * x + 1 - core, 0)
+                arrived(b * n_grp + 2 * x + 1 - core, 1)
+                tile(b, x)
+
+        for side in (-1, 1):
+            b = blk + side * (k - 2)
+            first = jnp.logical_or(k > 2, side > 0)
+
+            @pl.when(jnp.logical_and(jnp.logical_and(k > 1, first), inside(b)))
+            def _():
+                @pl.loop(1, n_x)
+                def _(dx):
+                    arrived(b * n_grp + 2 * x_at(dx) + 1 - core, 0)
+                    arrived(b * n_grp + 2 * x_at(dx) + 1 - core, 1)
+                    tile(b, x_at(dx))
 
         return 0
 
@@ -184,8 +210,9 @@
     r_buf[...] = r
     sq = r * r
     curv = slots[me, pl.ds(rank, rank), :] * h
-    stats[me, pl.ds(0, 8)] = jnp.sum(sq.reshape(rank // 8, 8, rows), axis=0)
-    stats[me, pl.ds(8, 8)] = jnp.sum(curv.reshape(rank // 8, 8, rows), axis=0)
+    sq = jnp.sum(sq.reshape(rank // 8, 8, rows), axis=0)
+    curv = jnp.sum(curv.reshape(rank // 8, 8, rows), axis=0)
+    stats[me] = jnp.concatenate([sq[:4] + sq[4:], curv[:4] + curv[4:]], axis=0)
 
     def to_stat(k):
         return pltpu.make_async_remote_copy(
@@ -208,8 +235,7 @@
             device_id_type=MESH,
         ).wait_recv()
 
-    @pl.loop(1, n_dev)
-    def _(k):
+    for k in range(1, n_dev):
         to_stat(k).start()
 
     store_h = pltpu.make_async_copy(h_buf, h_hbm, local_sem.at[0])
@@ -217,27 +243,36 @@
     store_h.start()
     store_r.start()
 
-    @pl.loop(1, n_blk)
-    def _(k):
-        to_z(k).wait_send()
+    for half in range(2):
+        for k, there in enumerate((blk - 1, blk + 1)):
+
+            @pl.when(inside(there))
+            def _():
+                to_z(blk, half, there, blk if k == 0 else n_blk).wait_send()
 
     @pl.loop(0, n_blk)
-    def _(k):
-        for dx in range(n_x):
-            if dx > 0:
-                to_x(k, dx).wait_send()
-            to_sibling(k, dx).wait_send()
-
-    @pl.loop(1, n_dev)
-    def _(k):
+    def _(b):
+        there = jnp.where(b < blk, blk + 1, blk - 1)
+
+        @pl.when(jnp.logical_and(b != blk, inside(there)))
+        def _():
+            for half in range(2):
+                to_z(b, half, there, b).wait_send()
+
+        for half in range(2):
+            for dx in range(n_x):
+                if dx > 0:
+                    to_x(b, dx, half).wait_send()
+                to_sibling(b, dx, half).wait_send()
+
+    for k in range(1, n_dev):
         stat_arrived(k)
 
     total = jnp.sum(stats[...], axis=0)
-    inner_ref[0] = jnp.sum(total[:8])
-    inner_ref[1] = jnp.sum(total[8:])
-
-    @pl.loop(1, n_dev)
-    def _(k):
+    inner_ref[0] = jnp.sum(total[:4])
+    inner_ref[1] = jnp.sum(total[4:])
+
+    for k in range(1, n_dev):
         to_stat(k).wait_send()
 
     store_h.wait()
@@ -263,12 +298,12 @@
             pltpu.VMEM((4 * rows, 2 * rank), jnp.float32),
             pltpu.VMEM((rank, rows), jnp.float32),
             pltpu.VMEM((rank, rows), jnp.float32),
-            pltpu.VMEM((n_dev, 16, rows), jnp.float32),
+            pltpu.VMEM((n_dev, 8, rows), jnp.float32),
             pltpu.SemaphoreType.DMA((3,)),
-            pltpu.SemaphoreType.DMA((n_blk,)),
-            pltpu.SemaphoreType.DMA((n_blk, n_x)),
-            pltpu.SemaphoreType.DMA((n_dev,)),
-            pltpu.SemaphoreType.DMA((n_dev,)),
+            pltpu.SemaphoreType.DMA((n_blk + 1, 2)),
+            pltpu.SemaphoreType.DMA((n_blk, n_x, 2)),
+            pltpu.SemaphoreType.DMA((n_dev, 2)),
+            pltpu.SemaphoreType.DMA((n_dev, 2)),
             pltpu.SemaphoreType.DMA((n_dev,)),
             pltpu.SemaphoreType.DMA((n_dev,)),
         ],

time: 29.4 us -> 29.2 us (level)
  no operation moved by 1% of the time
where the time goes in v2:
time: 29.2 us; the launch traced here: 29 us
  Pallas kernels  25.7 us (88%)
  local copies, waits for them, and re-layouts  2.57 us (9%)
  between operations  0.65 us (2%)
    pallas_call x1, Pallas kernels, local(): pl.pallas_call(functools.partial(kernel, n_blk, n_grp), out_shape=(flat,...  25.7 us
    unnamed x7, local copies, waits for them, and re-layouts  2.57 us

profile of v2, /device:TPU:0, one launch (start us, length us, event | category | flops | bytes accessed | tf_op | source)
XLA Modules:
  0.0 29.0 jit_solution(1377420012256840767)
XLA Ops:
  0.6 25.7 %shard_map.58 = (f32[64,128]{1,0:T(8,128)}, f32[64,128]{1,0:T(8,128)}, f32[2]{0:T(128)}) custom-call(f32[64,128]{1,0:T(8,128)} %f_hbm.1, f32[64,128]{1,0:T(8,128)} %t_hbm.1, s32[128,2048]{1,0:T(8,128)} %c_hbm.1), custom_call_target="tpu_custom_call" | custom-call | tf_op jit(solution)/shard_map/pallas_call | solution.py:289
  26.4 0.0 copy-start
  26.4 1.4 %copy.9 = f32[64,128]{1,0:T(8,128)} copy(f32[64,128]{1,0:T(8,128)} %get-tuple-element.6) | data formatting | bytes 65536
  27.8 0.0 copy-done
  27.8 0.0 copy-start.1
  27.8 0.6 %copy.10 = f32[64,128]{1,0:T(8,128)} copy(f32[64,128]{1,0:T(8,128)S(1)} %copy-done) | data formatting | bytes 65536
  28.4 0.1 copy-done.1
  28.5 0.5 %copy.11 = f32[2]{0:T(128)} copy(f32[2]{0:T(128)S(1)} %copy-done.1) | data formatting | bytes 16
Async XLA Ops:
  26.4 1.4 %copy-start = (f32[64,128]{1,0:T(8,128)S(1)}, f32[64,128]{1,0:T(8,128)}, u32[]{:S(2)}) copy-start(f32[64,128]{1,0:T(8,128)} %get-tuple-element.7) | copy-start | bytes 98308
  27.8 0.7 %copy-start.1 = (f32[2]{0:T(128)S(1)}, f32[2]{0:T(128)}, u32[]{:S(2)}) copy-start(f32[2]{0:T(128)} %get-tuple-element.8) | copy-start | bytes 28

commit v3 on v1

--- a/solution.py
+++ b/solution.py
@@ -50,9 +50,16 @@
     me = blk * n_grp + grp
     sibling = 2 * x + 1 - core
 
-    def peer(k):
-        there = lax.rem(me + k, n_dev)
-        return there, {"blk": there // n_grp, "grp": lax.rem(there, n_grp)}
+    pairs, pair, odd = n_blk // 2, blk // 2, lax.rem(blk, 2)
+
+    def x_at(dx):
+        return lax.rem(x + dx, n_x)
+
+    def target(e):
+        return lax.rem(pair + e // 2, pairs) * 2 + lax.rem(odd + e, 2)
+
+    def source(e):
+        return lax.rem(pair + pairs - e // 2, pairs) * 2 + lax.rem(odd + e, 2)
 
     load_f = pltpu.make_async_copy(f_hbm, slots.at[me, pl.ds(0, rank)], local_sem.at[0])
     load_t = pltpu.make_async_copy(t_hbm, slots.at[me, pl.ds(rank, rank)], local_sem.at[1])
@@ -63,13 +70,22 @@
 
     barrier = pltpu.get_barrier_semaphore()
 
-    @pl.loop(1, n_dev)
-    def _(k):
-        pl.semaphore_signal(barrier, inc=1, device_id=peer(k)[1], device_id_type=MESH)
+    friends = [(e, 0) for e in range(n_blk - 1, 0, -1)]
+    friends += [(e, dx) for e in (1, 0) for dx in range(1, n_x)]
+    for e, dx in friends:
+        pl.semaphore_signal(
+            barrier,
+            inc=1,
+            device_id={"blk": target(e), "grp": 2 * x_at(dx) + core},
+            device_id_type=MESH,
+        )
+    pl.semaphore_signal(
+        barrier, inc=1, device_id={"blk": blk, "grp": sibling}, device_id_type=MESH
+    )
 
     load_f.wait()
     load_t.wait()
-    pl.semaphore_wait(barrier, n_dev - 1)
+    pl.semaphore_wait(barrier, len(friends) + 1)
 
     def send(slot, b, g, sem):
         return pltpu.make_async_remote_copy(
@@ -81,34 +97,31 @@
             device_id_type=MESH,
         )
 
-    def arrived(slot):
-        send(slot, blk, sibling, s_sem.at[0]).wait_recv()
-
-    def to_z(k):
-        return send(me, lax.rem(blk + k, n_blk), grp, z_sem.at[k])
-
-    def from_z(k):
-        return lax.rem(blk + n_blk - k, n_blk)
-
-    def x_at(dx):
-        return lax.rem(x + dx, n_x)
-
-    def to_x(k, dx):
-        return send(from_z(k) * n_grp + grp, blk, 2 * x_at(dx) + core, x_sem.at[k, dx])
-
-    def to_sibling(k, dx):
-        return send(from_z(k) * n_grp + 2 * x_at(dx) + core, blk, sibling, s_sem.at[k * n_x + dx])
-
-    def slot_own_core(k, dx):
-        return from_z(k) * n_grp + 2 * x_at(dx) + core
-
-    def slot_sibling(k, dx):
-        return from_z(k) * n_grp + 2 * x_at(dx) + 1 - core
-
-    for k in range(1, n_blk):
-        to_z(k).start()
+    def slot_at(e, dx, c):
+        return source(e) * n_grp + 2 * x_at(dx) + c
+
+    def arrived(e, dx, c):
+        send(slot_at(e, dx, c), blk, sibling, s_sem.at[0]).wait_recv()
+
+    def to_z(e):
+        return send(me, target(e), grp, z_sem.at[e])
+
+    def to_x(e, dx):
+        there = 2 * x_at(dx) + core
+        if isinstance(e, int) and e < 2:
+            return send(me, target(e), there, x_sem.at[e, dx])
+        return send(slot_at(e, 0, core), blk, there, x_sem.at[e, dx])
+
+    def to_sibling(e, dx):
+        return send(slot_at(e, dx, core), blk, sibling, s_sem.at[e * n_x + dx])
+
+    for e in range(2, n_blk):
+        to_z(e).start()
     for dx in range(1, n_x):
         to_x(0, dx).start()
+    to_z(1).start()
+    for dx in range(1, n_x):
+        to_x(1, dx).start()
     to_sibling(0, 0).start()
 
     u = slots[me, pl.ds(0, rank), :]
@@ -146,34 +159,49 @@
             p, uu, (((1,), (1,)), ((), ())), preferred_element_type=jnp.float32
         )
 
-    def step(k, _):
-        @pl.when(k < n_blk)
+    def own_tile(e):
+        arrived(e, 0, 1 - core)
+        tile(source(e), x)
+
+    def other_tiles(e):
+        @pl.loop(1, n_x)
+        def _(dx):
+            arrived(e, dx, 1 - core)
+            tile(source(e), x_at(dx))
+
+    def pass_x(e):
+        for dx in range(1, n_x):
+            arrived(e, dx, core)
+            to_sibling(e, dx).start()
+
+    own_tile(0)
+    pass_x(0)
+    arrived(1, 0, core)
+    to_sibling(1, 0).start()
+    pass_x(1)
+
+    @pl.loop(2, n_blk)
+    def _(e):
+        arrived(e, 0, core)
+        for dx in range(1, n_x):
+            to_x(e, dx).start()
+        to_sibling(e, 0).start()
+
+        @pl.when(e == 2)
         def _():
-            @pl.when(k > 0)
-            def _():
-                arrived(slot_own_core(k, 0))
-                for dx in range(1, n_x):
-                    to_x(k, dx).start()
-                to_sibling(k, 0).start()
-
-        @pl.when(jnp.logical_and(k > 0, k <= n_blk))
-        def _():
-            for dx in range(1, n_x):
-                arrived(slot_own_core(k - 1, dx))
-                to_sibling(k - 1, dx).start()
-            arrived(slot_sibling(k - 1, 0))
-            tile(from_z(k - 1), x)
-
-        @pl.when(k > 1)
-        def _():
-            @pl.loop(1, n_x)
-            def _(dx):
-                arrived(slot_sibling(k - 2, dx))
-                tile(from_z(k - 2), x_at(dx))
-
-        return 0
-
-    lax.fori_loop(0, n_blk + 2, step, 0)
+            other_tiles(0)
+
+    own_tile(1)
+    other_tiles(1)
+
+    @pl.loop(2, n_blk)
+    def _(e):
+        own_tile(e)
+        pass_x(e)
+
+    @pl.loop(2, n_blk)
+    def _(e):
+        other_tiles(e)
 
     scale = 1.0 / jnp.sqrt(jnp.float32(nodes))
     h = (acc[pl.ds(0, rows)] + acc[pl.ds(rows, rows)]).T
@@ -184,32 +212,33 @@
     r_buf[...] = r
     sq = r * r
     curv = slots[me, pl.ds(rank, rank), :] * h
-    stats[me, pl.ds(0, 8)] = jnp.sum(sq.reshape(rank // 8, 8, rows), axis=0)
-    stats[me, pl.ds(8, 8)] = jnp.sum(curv.reshape(rank // 8, 8, rows), axis=0)
-
-    def to_stat(k):
+    sq = jnp.sum(sq.reshape(rank // 8, 8, rows), axis=0)
+    curv = jnp.sum(curv.reshape(rank // 8, 8, rows), axis=0)
+    stats[me] = jnp.concatenate([sq[:4] + sq[4:], curv[:4] + curv[4:]], axis=0)
+
+    others = [
+        (e, dx, c) for e in range(n_blk - 1, -1, -1) for dx in range(n_x - 1, -1, -1) for c in range(2)
+    ][:-1]
+
+    def stat(slot, b, g, k):
         return pltpu.make_async_remote_copy(
-            src_ref=stats.at[me],
-            dst_ref=stats.at[me],
+            src_ref=stats.at[slot],
+            dst_ref=stats.at[slot],
             send_sem=stat_send.at[k],
-            recv_sem=stat_recv.at[me],
-            device_id=peer(k)[1],
+            recv_sem=stat_recv.at[slot],
+            device_id={"blk": b, "grp": g},
             device_id_type=MESH,
         )
 
+    def to_stat(k):
+        e, dx, c = others[k]
+        return stat(me, target(e), 2 * x_at(dx) + lax.rem(core + 1 - c, 2), k)
+
     def stat_arrived(k):
-        there = peer(k)[0]
-        pltpu.make_async_remote_copy(
-            src_ref=stats.at[there],
-            dst_ref=stats.at[there],
-            send_sem=stat_send.at[0],
-            recv_sem=stat_recv.at[there],
-            device_id=peer(k)[1],
-            device_id_type=MESH,
-        ).wait_recv()
-
-    @pl.loop(1, n_dev)
-    def _(k):
+        e, dx, c = others[k]
+        stat(slot_at(e, dx, lax.rem(core + 1 - c, 2)), blk, sibling, 0).wait_recv()
+
+    for k in range(n_dev - 1):
         to_stat(k).start()
 
     store_h = pltpu.make_async_copy(h_buf, h_hbm, local_sem.at[0])
@@ -217,27 +246,22 @@
     store_h.start()
     store_r.start()
 
-    @pl.loop(1, n_blk)
-    def _(k):
-        to_z(k).wait_send()
-
-    @pl.loop(0, n_blk)
-    def _(k):
+    for e in range(1, n_blk):
+        to_z(e).wait_send()
+    for e in range(n_blk):
         for dx in range(n_x):
             if dx > 0:
-                to_x(k, dx).wait_send()
-            to_sibling(k, dx).wait_send()
-
-    @pl.loop(1, n_dev)
-    def _(k):
+                to_x(e, dx).wait_send()
+            to_sibling(e, dx).wait_send()
+
+    for k in range(n_dev - 1):
         stat_arrived(k)
 
     total = jnp.sum(stats[...], axis=0)
-    inner_ref[0] = jnp.sum(total[:8])
-    inner_ref[1] = jnp.sum(total[8:])
-
-    @pl.loop(1, n_dev)
-    def _(k):
+    inner_ref[0] = jnp.sum(total[:4])
+    inner_ref[1] = jnp.sum(total[4:])
+
+    for k in range(n_dev - 1):
         to_stat(k).wait_send()
 
     store_h.wait()
@@ -263,11 +287,11 @@
             pltpu.VMEM((4 * rows, 2 * rank), jnp.float32),
             pltpu.VMEM((rank, rows), jnp.float32),
             pltpu.VMEM((rank, rows), jnp.float32),
-            pltpu.VMEM((n_dev, 16, rows), jnp.float32),
+            pltpu.VMEM((n_dev, 8, rows), jnp.float32),
             pltpu.SemaphoreType.DMA((3,)),
             pltpu.SemaphoreType.DMA((n_blk,)),
             pltpu.SemaphoreType.DMA((n_blk, n_x)),
-            pltpu.SemaphoreType.DMA((n_dev,)),
+            pltpu.SemaphoreType.DMA((n_blk * n_x,)),
             pltpu.SemaphoreType.DMA((n_dev,)),
             pltpu.SemaphoreType.DMA((n_dev,)),
             pltpu.SemaphoreType.DMA((n_dev,)),

time: 29.4 us -> 26.5 us (0.901)
  Pallas kernels: 25.9 us -> 23.1 us
    pallas_call x1, Pallas kernels: 25.9 us -> 23.1 us  [local(): pl.pallas_call(functools.partial(kernel, n_blk, n_grp), out_shape=(flat,...]
where the time goes in v3:
time: 26.5 us; the launch traced here: 26.3 us
  Pallas kernels  23.1 us (87%)
  local copies, waits for them, and re-layouts  2.57 us (10%)
  between operations  0.65 us (2%)
    pallas_call x1, Pallas kernels, local(): pl.pallas_call(functools.partial(kernel, n_blk, n_grp), out_shape=(flat,...  23.1 us
    unnamed x7, local copies, waits for them, and re-layouts  2.57 us

profile of v3, /device:TPU:0, one launch (start us, length us, event | category | flops | bytes accessed | tf_op | source)
XLA Modules:
  0.0 26.3 jit_solution(145405050326396474)
XLA Ops:
  0.6 23.1 %shard_map.58 = (f32[64,128]{1,0:T(8,128)}, f32[64,128]{1,0:T(8,128)}, f32[2]{0:T(128)}) custom-call(f32[64,128]{1,0:T(8,128)} %f_hbm.1, f32[64,128]{1,0:T(8,128)} %t_hbm.1, s32[128,2048]{1,0:T(8,128)} %c_hbm.1), custom_call_target="tpu_custom_call" | custom-call | tf_op jit(solution)/shard_map/pallas_call | solution.py:278
  23.7 0.0 copy-start
  23.7 1.4 %copy.9 = f32[64,128]{1,0:T(8,128)} copy(f32[64,128]{1,0:T(8,128)} %get-tuple-element.6) | data formatting | bytes 65536
  25.1 0.0 copy-done
  25.1 0.0 copy-start.1
  25.1 0.6 %copy.10 = f32[64,128]{1,0:T(8,128)} copy(f32[64,128]{1,0:T(8,128)S(1)} %copy-done) | data formatting | bytes 65536
  25.7 0.1 copy-done.1
  25.8 0.5 %copy.11 = f32[2]{0:T(128)} copy(f32[2]{0:T(128)S(1)} %copy-done.1) | data formatting | bytes 16
Async XLA Ops:
  23.7 1.4 %copy-start = (f32[64,128]{1,0:T(8,128)S(1)}, f32[64,128]{1,0:T(8,128)}, u32[]{:S(2)}) copy-start(f32[64,128]{1,0:T(8,128)} %get-tuple-element.7) | copy-start | bytes 98308
  25.1 0.7 %copy-start.1 = (f32[2]{0:T(128)S(1)}, f32[2]{0:T(128)}, u32[]{:S(2)}) copy-start(f32[2]{0:T(128)} %get-tuple-element.8) | copy-start | bytes 28

commit v4 on v3

--- a/solution.py
+++ b/solution.py
@@ -22,15 +22,12 @@
     f_hbm,
     t_hbm,
     c_hbm,
-    h_hbm,
-    r_hbm,
-    inner_ref,
+    out_hbm,
     slots,
     counts,
     lhs,
     acc,
-    h_buf,
-    r_buf,
+    out_buf,
     stats,
     local_sem,
     z_sem,
@@ -42,7 +39,7 @@
 ):
     n_x = n_grp // 2
     n_dev = n_blk * n_grp
-    rank, rows = h_buf.shape
+    rank, rows = f_hbm.shape
     nodes = counts.shape[1]
     blk = lax.axis_index("blk")
     grp = lax.axis_index("grp")
@@ -70,8 +67,8 @@
 
     barrier = pltpu.get_barrier_semaphore()
 
-    friends = [(e, 0) for e in range(n_blk - 1, 0, -1)]
-    friends += [(e, dx) for e in (1, 0) for dx in range(1, n_x)]
+    friends = [(e, 0) for e in range(2, n_blk, 2)]
+    friends += [(e, dx) for e in (1, 0) for dx in range(1 - e, n_x)]
     for e, dx in friends:
         pl.semaphore_signal(
             barrier,
@@ -107,15 +104,20 @@
         return send(me, target(e), grp, z_sem.at[e])
 
     def to_x(e, dx):
-        there = 2 * x_at(dx) + core
-        if isinstance(e, int) and e < 2:
-            return send(me, target(e), there, x_sem.at[e, dx])
-        return send(slot_at(e, 0, core), blk, there, x_sem.at[e, dx])
+        return send(me, target(e), 2 * x_at(dx) + core, x_sem.at[e, dx])
+
+    def relay(e):
+        slot = slot_at(e, 0, core)
+        return [
+            send(slot, b, 2 * x_at(dx) + core, x_sem.at[e, dx + n_x * k])
+            for k, b in ((1, target(1)), (0, blk))
+            for dx in range(n_x - 1, -k, -1)
+        ]
 
     def to_sibling(e, dx):
         return send(slot_at(e, dx, core), blk, sibling, s_sem.at[e * n_x + dx])
 
-    for e in range(2, n_blk):
+    for e in range(2, n_blk, 2):
         to_z(e).start()
     for dx in range(1, n_x):
         to_x(0, dx).start()
@@ -180,36 +182,38 @@
     to_sibling(1, 0).start()
     pass_x(1)
 
-    @pl.loop(2, n_blk)
-    def _(e):
-        arrived(e, 0, core)
-        for dx in range(1, n_x):
-            to_x(e, dx).start()
-        to_sibling(e, 0).start()
-
-        @pl.when(e == 2)
-        def _():
-            other_tiles(0)
-
+    @pl.loop(1, pairs)
+    def _(m):
+        arrived(2 * m, 0, core)
+        for copy in relay(2 * m):
+            copy.start()
+        to_sibling(2 * m, 0).start()
+
+    other_tiles(0)
     own_tile(1)
     other_tiles(1)
 
-    @pl.loop(2, n_blk)
-    def _(e):
-        own_tile(e)
-        pass_x(e)
-
-    @pl.loop(2, n_blk)
-    def _(e):
-        other_tiles(e)
+    @pl.loop(1, pairs)
+    def _(m):
+        own_tile(2 * m)
+        pass_x(2 * m)
+        arrived(2 * m + 1, 0, core)
+        to_sibling(2 * m + 1, 0).start()
+        pass_x(2 * m + 1)
+
+    @pl.loop(1, pairs)
+    def _(m):
+        other_tiles(2 * m)
+        own_tile(2 * m + 1)
+        other_tiles(2 * m + 1)
 
     scale = 1.0 / jnp.sqrt(jnp.float32(nodes))
     h = (acc[pl.ds(0, rows)] + acc[pl.ds(rows, rows)]).T
     r = (acc[pl.ds(2 * rows, rows)] + acc[pl.ds(3 * rows, rows)]).T
     h = (h[:rank] + h[rank:]) * scale
     r = (r[:rank] + r[rank:]) * scale
-    h_buf[...] = h
-    r_buf[...] = r
+    out_buf[pl.ds(0, rank)] = h
+    out_buf[pl.ds(rank, rank)] = r
     sq = r * r
     curv = slots[me, pl.ds(rank, rank), :] * h
     sq = jnp.sum(sq.reshape(rank // 8, 8, rows), axis=0)
@@ -241,31 +245,46 @@
     for k in range(n_dev - 1):
         to_stat(k).start()
 
-    store_h = pltpu.make_async_copy(h_buf, h_hbm, local_sem.at[0])
-    store_r = pltpu.make_async_copy(r_buf, r_hbm, local_sem.at[1])
-    store_h.start()
-    store_r.start()
-
-    for e in range(1, n_blk):
+    top, end = pl.ds(0, 2 * rank), pl.ds(2 * rank, 8)
+    store = pltpu.make_async_copy(out_buf.at[top], out_hbm.at[top], local_sem.at[0])
+    store_sums = pltpu.make_async_copy(out_buf.at[end], out_hbm.at[end], local_sem.at[1])
+    store.start()
+
+    to_z(1).wait_send()
+    for e in range(2, n_blk, 2):
         to_z(e).wait_send()
+        for copy in relay(e):
+            copy.wait_send()
+    for e in range(2):
+        for dx in range(1, n_x):
+            to_x(e, dx).wait_send()
     for e in range(n_blk):
         for dx in range(n_x):
-            if dx > 0:
-                to_x(e, dx).wait_send()
             to_sibling(e, dx).wait_send()
 
     for k in range(n_dev - 1):
         stat_arrived(k)
 
     total = jnp.sum(stats[...], axis=0)
-    inner_ref[0] = jnp.sum(total[:4])
-    inner_ref[1] = jnp.sum(total[4:])
+    sums = jnp.where(
+        lax.broadcasted_iota(jnp.int32, (8, rows), 1) == 0, jnp.sum(total[:4]), jnp.sum(total[4:])
+    )
+    out_buf[end] = sums
+    store_sums.start()
 
     for k in range(n_dev - 1):
         to_stat(k).wait_send()
 
-    store_h.wait()
-    store_r.wait()
+    store.wait()
+    store_sums.wait()
+
+
+def unpack(packed, h_ref, r_ref, inner_ref):
+    rank = h_ref.shape[0]
+    h_ref[...] = packed[pl.ds(0, rank)]
+    r_ref[...] = packed[pl.ds(rank, rank)]
+    inner_ref[0] = packed[2 * rank, 0]
+    inner_ref[1] = packed[2 * rank, 1]
 
 
 def local(n_blk, n_grp, factors, tangent, counts):
@@ -274,23 +293,21 @@
     n_x = n_grp // 2
     n_dev = n_blk * n_grp
     anyspace = pl.BlockSpec(memory_space=pl.ANY)
-    flat = jax.ShapeDtypeStruct((rank, rows), jnp.float32)
-    return pl.pallas_call(
+    packed = pl.pallas_call(
         functools.partial(kernel, n_blk, n_grp),
-        out_shape=(flat, flat, jax.ShapeDtypeStruct((2,), jnp.float32)),
+        out_shape=jax.ShapeDtypeStruct((2 * rank + 8, rows), jnp.float32),
         in_specs=[anyspace] * 3,
-        out_specs=(anyspace, anyspace, pl.BlockSpec(memory_space=pltpu.SMEM)),
+        out_specs=anyspace,
         scratch_shapes=[
             pltpu.VMEM((n_dev, 2 * rank, rows), jnp.float32),
             pltpu.VMEM((rows, nodes), jnp.int32),
             pltpu.VMEM((4 * rows, 4 * rank), jnp.bfloat16),
             pltpu.VMEM((4 * rows, 2 * rank), jnp.float32),
-            pltpu.VMEM((rank, rows), jnp.float32),
-            pltpu.VMEM((rank, rows), jnp.float32),
+            pltpu.VMEM((2 * rank + 8, rows), jnp.float32),
             pltpu.VMEM((n_dev, 8, rows), jnp.float32),
             pltpu.SemaphoreType.DMA((3,)),
             pltpu.SemaphoreType.DMA((n_blk,)),
-            pltpu.SemaphoreType.DMA((n_blk, n_x)),
+            pltpu.SemaphoreType.DMA((n_blk, 2 * n_x)),
             pltpu.SemaphoreType.DMA((n_blk * n_x,)),
             pltpu.SemaphoreType.DMA((n_dev,)),
             pltpu.SemaphoreType.DMA((n_dev,)),
@@ -300,6 +317,13 @@
             collective_id=0, has_side_effects=True, vmem_limit_bytes=64 * 1024 * 1024 - 64 * 1024
         ),
     )(factors, tangent, counts)
+    flat = jax.ShapeDtypeStruct((rank, rows), jnp.float32)
+    return pl.pallas_call(
+        unpack,
+        out_shape=(flat, flat, jax.ShapeDtypeStruct((2,), jnp.float32)),
+        in_specs=[pl.BlockSpec(memory_space=pltpu.VMEM)],
+        out_specs=(pl.BlockSpec(memory_space=pltpu.VMEM), pl.BlockSpec(memory_space=pltpu.VMEM), pl.BlockSpec(memory_space=pltpu.SMEM)),
+    )(packed)
 
 
 def solution(mesh):

time: 26.5 us -> 25 us (0.943)
  local copies, waits for them, and re-layouts: 2.57 us -> 0 us
  Pallas kernels: 23.1 us -> 24.2 us
    unnamed x7 -> x0, local copies, waits for them, and re-layouts: 2.57 us -> none
    pallas_call x1 -> x2, Pallas kernels: 23.1 us -> 24.2 us  [the longest x1 22.7 us: local(): pl.pallas_call(functools.partial(kernel, n_blk, n_grp), out_shape=jax.Sha...]
where the time goes in v4:
time: 25 us; the launch traced here: 24.8 us
  Pallas kernels  24.2 us (97%)
  between operations  0.64 us (3%)
    pallas_call x1, Pallas kernels, local(): pl.pallas_call(functools.partial(kernel, n_blk, n_grp), out_shape=jax.Sha...  22.7 us
    pallas_call x1, Pallas kernels, local(): pl.pallas_call(unpack, out_shape=(flat, flat, jax.ShapeDtypeStruct((2,),...  1.52 us

profile of v4, /device:TPU:0, one launch (start us, length us, event | category | flops | bytes accessed | tf_op | source)
XLA Modules:
  0.0 24.8 jit_solution(1960626495526440272)
XLA Ops:
  0.6 22.7 %shard_map.58.packed = f32[136,128]{1,0:T(8,128)} custom-call(f32[64,128]{1,0:T(8,128)} %f_hbm.1, f32[64,128]{1,0:T(8,128)} %t_hbm.1, s32[128,2048]{1,0:T(8,128)} %c_hbm.1), custom_call_target="tpu_custom_call" | custom-call | tf_op jit(solution)/shard_map/pallas_call | solution.py:296
  23.3 1.5 %shard_map.59 = (f32[64,128]{1,0:T(8,128)}, f32[64,128]{1,0:T(8,128)}, f32[2]{0:T(128)}) custom-call(f32[136,128]{1,0:T(8,128)} %shard_map.58.packed), custom_call_target="tpu_custom_call" | custom-call | tf_op jit(solution)/shard_map/pallas_call | solution.py:321

commit v5 on v4

--- a/solution.py
+++ b/solution.py
@@ -178,16 +178,16 @@
 
     own_tile(0)
     pass_x(0)
-    arrived(1, 0, core)
-    to_sibling(1, 0).start()
-    pass_x(1)
-
     @pl.loop(1, pairs)
     def _(m):
         arrived(2 * m, 0, core)
         for copy in relay(2 * m):
             copy.start()
         to_sibling(2 * m, 0).start()
+
+    arrived(1, 0, core)
+    to_sibling(1, 0).start()
+    pass_x(1)
 
     other_tiles(0)
     own_tile(1)

time: 25 us -> 24 us (0.960)
  Pallas kernels: 24.2 us -> 23.2 us
    pallas_call x1, Pallas kernels: 22.7 us -> 21.7 us  [local(): pl.pallas_call(functools.partial(kernel, n_blk, n_grp), out_shape=jax.Sha...]
where the time goes in v5:
time: 24 us; the launch traced here: 23.8 us
  Pallas kernels  23.2 us (97%)
  between operations  0.64 us (3%)
    pallas_call x1, Pallas kernels, local(): pl.pallas_call(functools.partial(kernel, n_blk, n_grp), out_shape=jax.Sha...  21.7 us
    pallas_call x1, Pallas kernels, local(): pl.pallas_call(unpack, out_shape=(flat, flat, jax.ShapeDtypeStruct((2,),...  1.52 us

profile of v5, /device:TPU:0, one launch (start us, length us, event | category | flops | bytes accessed | tf_op | source)
XLA Modules:
  0.0 23.8 jit_solution(10783045857175508462)
XLA Ops:
  0.6 21.7 %shard_map.58.packed = f32[136,128]{1,0:T(8,128)} custom-call(f32[64,128]{1,0:T(8,128)} %f_hbm.1, f32[64,128]{1,0:T(8,128)} %t_hbm.1, s32[128,2048]{1,0:T(8,128)} %c_hbm.1), custom_call_target="tpu_custom_call" | custom-call | tf_op jit(solution)/shard_map/pallas_call | solution.py:296
  22.3 1.5 %shard_map.59 = (f32[64,128]{1,0:T(8,128)}, f32[64,128]{1,0:T(8,128)}, f32[2]{0:T(128)}) custom-call(f32[136,128]{1,0:T(8,128)} %shard_map.58.packed), custom_call_target="tpu_custom_call" | custom-call | tf_op jit(solution)/shard_map/pallas_call | solution.py:321

commit v6 on v5

--- a/solution.py
+++ b/solution.py
@@ -191,18 +191,19 @@
 
     other_tiles(0)
     own_tile(1)
-    other_tiles(1)
 
     @pl.loop(1, pairs)
     def _(m):
-        own_tile(2 * m)
         pass_x(2 * m)
         arrived(2 * m + 1, 0, core)
         to_sibling(2 * m + 1, 0).start()
         pass_x(2 * m + 1)
 
+    other_tiles(1)
+
     @pl.loop(1, pairs)
     def _(m):
+        own_tile(2 * m)
         other_tiles(2 * m)
         own_tile(2 * m + 1)
         other_tiles(2 * m + 1)

time: 24 us -> 24 us (level)
  no operation moved by 1% of the time
where the time goes in v6:
time: 24 us; the launch traced here: 23.8 us
  Pallas kernels  23.2 us (97%)
  between operations  0.64 us (3%)
    pallas_call x1, Pallas kernels, local(): pl.pallas_call(functools.partial(kernel, n_blk, n_grp), out_shape=jax.Sha...  21.7 us
    pallas_call x1, Pallas kernels, local(): pl.pallas_call(unpack, out_shape=(flat, flat, jax.ShapeDtypeStruct((2,),...  1.52 us

profile of v6, /device:TPU:0, one launch (start us, length us, event | category | flops | bytes accessed | tf_op | source)
XLA Modules:
  0.0 23.8 jit_solution(10102108956108064262)
XLA Ops:
  0.6 21.7 %shard_map.58.packed = f32[136,128]{1,0:T(8,128)} custom-call(f32[64,128]{1,0:T(8,128)} %f_hbm.1, f32[64,128]{1,0:T(8,128)} %t_hbm.1, s32[128,2048]{1,0:T(8,128)} %c_hbm.1), custom_call_target="tpu_custom_call" | custom-call | tf_op jit(solution)/shard_map/pallas_call | solution.py:297
  22.3 1.5 %shard_map.59 = (f32[64,128]{1,0:T(8,128)}, f32[64,128]{1,0:T(8,128)}, f32[2]{0:T(128)}) custom-call(f32[136,128]{1,0:T(8,128)} %shard_map.58.packed), custom_call_target="tpu_custom_call" | custom-call | tf_op jit(solution)/shard_map/pallas_call | solution.py:322
